TPU v7x, 32 devices: a whole 2x2x4 slice. The times are simulated.
32 devices in a mesh: seq: 8 (over z, y), tp: 2 (over core), pp: 2 (over x).
Axes of the slice: x: 2, y: 2, z: 4, core: 2. Of those that a mesh axis runs over, the one named last changes fastest.
Arguments:
- queries: bfloat16 [2, 4096, 4096], P('pp', 'seq', 'tp'), may hold values from -1.796875 to 1.796875
- keys: bfloat16 [2, 4096, 4096], P('pp', 'seq', 'tp'), may hold values from -1.796875 to 1.796875
- values: bfloat16 [2, 4096, 4096], P('pp', 'seq', 'tp'), may hold values from -25.375 to 25.375
- upstream: bfloat16 [2, 4096, 3072], P('pp', 'seq', 'tp'), may hold values from -6 to 6
- out_weight: bfloat16 [2, 4096, 3072], P('pp', 'tp'), may hold values from -0.09375 to 0.09375
- gain: float32 [2, 4096], P('pp', 'tp'), may hold values from 0.25 to 1.75
- log_decay: float32 [2, 32, 4096], P('pp', 'tp', 'seq'), may hold values from -0.7 to 0
Outputs:
- grad_queries: bfloat16 [2, 4096, 4096], P('pp', 'seq', 'tp')
- grad_keys: bfloat16 [2, 4096, 4096], P('pp', 'seq', 'tp')
- grad_values: bfloat16 [2, 4096, 4096], P('pp', 'seq', 'tp')
All inputs are finite; a program needn't handle non-finite values.
Results may differ from a plain program's by a relative error of at most 0.014.
Values may be sent and summed in bfloat16 or wider, within the bound.
A program may use at most 128 MiB of HBM per device.

v0:
```python
import jax
import jax.numpy as jnp
from jax import lax
from jax.sharding import PartitionSpec as P

HEAD = 128


EPS = 1e-06


def from_behind(value, axis, steps):
    count = lax.axis_size(axis)
    pairs = [(source, (source + steps) % count) for source in range(count)]
    return lax.ppermute(value, axis, pairs)


def carried_in(value, axis, combine, identity):
    devices, index = (lax.axis_size(axis), lax.axis_index(axis))
    everything = jax.tree.map(
        lambda part, kind: lax.all_gather(part.astype(kind), axis),
        value,
        (jnp.bfloat16, jnp.bfloat16),
    )
    start = jax.tree.map(
        lambda part, zero: jnp.broadcast_to(jnp.asarray(zero, part.dtype), part.shape),
        value,
        identity,
    )

    def lap(k, before):
        at = devices - 1 - k
        reached = at > index
        new = combine(
            before, jax.tree.map(lambda part, own: part[at].astype(own.dtype), everything, value)
        )
        return jax.tree.map(lambda a, b: jnp.where(reached, a, b), new, before)

    return lax.fori_loop(0, devices, lap, start)


def linked(earlier, later_part):
    return (
        earlier[0] + later_part[0],
        jnp.exp(later_part[0])[:, None, None] * earlier[1] + later_part[1],
    )


def local(queries, keys, values, upstream, out_weight, gain, log_decay):
    tokens = queries.shape[1]
    local_width = queries.shape[2]
    heads_here = local_width // HEAD
    features = local_width * lax.axis_size("tp")
    query_rows = queries[0].reshape(tokens, heads_here, HEAD)
    key_rows = keys[0].reshape(tokens, heads_here, HEAD)
    value_rows = values[0].reshape(tokens, heads_here, HEAD)
    cumulative = jnp.cumsum(log_decay[0], axis=1)
    block_total = cumulative[:, -1]
    row_ids = lax.broadcasted_iota(jnp.int32, (tokens, tokens), 0)
    col_ids = lax.broadcasted_iota(jnp.int32, (tokens, tokens), 1)
    causal = (row_ids >= col_ids)[None]
    spread = cumulative[:, :, None] - cumulative[:, None, :]
    decay_mat = jnp.where(causal, jnp.exp(jnp.where(causal, spread, 0.0)), 0.0)
    scores = jnp.einsum("thd,shd->hts", query_rows, key_rows, preferred_element_type=jnp.float32)
    masked = (scores * decay_mat).astype(jnp.bfloat16)
    tail_decay = jnp.exp(block_total[:, None] - cumulative).T
    head_decay = jnp.exp(cumulative).T
    weighted_keys = (key_rows * tail_decay[:, :, None]).astype(jnp.bfloat16)
    local_state = jnp.einsum(
        "thd,the->hde", weighted_keys, value_rows, preferred_element_type=jnp.float32
    )
    zero_state = jnp.zeros((heads_here, HEAD, HEAD), jnp.float32)
    all_totals = lax.all_gather(block_total[None], "seq", axis=0, tiled=True)
    own_index = lax.axis_index("seq")
    running = jnp.cumsum(all_totals, axis=0)
    before = lax.dynamic_index_in_dim(running, own_index, 0, keepdims=False) - block_total
    pieces = lax.all_gather(
        local_state[None].astype(jnp.bfloat16), "seq", axis=0, tiled=True
    ).astype(jnp.float32)
    shard_count = pieces.shape[0]
    positions = jnp.arange(shard_count, dtype=jnp.int32)
    earlier = (positions < own_index)[:, None]
    weight = jnp.where(earlier, jnp.exp(jnp.where(earlier, before[None, :] - running, 0.0)), 0.0)
    state_in = zero_state + jnp.sum(weight[:, :, None, None] * pieces, axis=0)
    state_bf = state_in.astype(jnp.bfloat16)
    attended = jnp.einsum("hts,shd->thd", masked, value_rows, preferred_element_type=jnp.float32)
    attended = attended + head_decay[:, :, None] * jnp.einsum(
        "thd,hde->the", query_rows, state_bf, preferred_element_type=jnp.float32
    )
    flat_out = attended.reshape(tokens, local_width)
    squares = jnp.sum(flat_out * flat_out, axis=1)
    square_total = lax.psum(squares, "tp")
    received = from_behind(upstream, "pp", -1)
    weight_rows = out_weight[0]
    grad_hidden = lax.dot_general(
        lax.all_gather(received[0], "tp", axis=1, tiled=True),
        weight_rows,
        (((1,), (1,)), ((), ())),
        preferred_element_type=jnp.float32,
    )
    grad_norm = grad_hidden * gain[0][None, :]
    crossed = jnp.sum(grad_norm * flat_out, axis=1)
    cross_total = lax.psum(crossed, "tp")
    inverse = 1.0 / jnp.sqrt(square_total / features + EPS)
    factor = inverse * inverse * inverse * (cross_total / features)
    grad_attn = (inverse[:, None] * grad_norm - factor[:, None] * flat_out).astype(jnp.bfloat16)
    grad_attn = grad_attn.reshape(tokens, heads_here, HEAD)
    dscore = jnp.einsum("thd,shd->hts", grad_attn, value_rows, preferred_element_type=jnp.float32)
    dmask = (dscore * decay_mat).astype(jnp.bfloat16)
    weighted_queries = (query_rows * head_decay[:, :, None]).astype(jnp.bfloat16)
    passed = jnp.einsum(
        "thd,the->hde", weighted_queries, grad_attn, preferred_element_type=jnp.float32
    )
    later_state = carried_in(
        (block_total, passed), "seq", linked, (jnp.zeros_like(block_total), zero_state)
    )[1]
    later_bf = later_state.astype(jnp.bfloat16)
    grad_q = jnp.einsum("hts,shd->thd", dmask, key_rows, preferred_element_type=jnp.float32)
    grad_q = grad_q + head_decay[:, :, None] * jnp.einsum(
        "the,hde->thd", grad_attn, state_bf, preferred_element_type=jnp.float32
    )
    grad_k = jnp.einsum("hts,thd->shd", dmask, query_rows, preferred_element_type=jnp.float32)
    grad_k = grad_k + tail_decay[:, :, None] * jnp.einsum(
        "the,hde->thd", value_rows, later_bf, preferred_element_type=jnp.float32
    )
    grad_v = jnp.einsum("hts,thd->shd", masked, grad_attn, preferred_element_type=jnp.float32)
    grad_v = grad_v + tail_decay[:, :, None] * jnp.einsum(
        "thd,hde->the", key_rows, later_bf, preferred_element_type=jnp.float32
    )
    out_shape = (1, tokens, local_width)
    return (
        grad_q.astype(jnp.bfloat16).reshape(out_shape),
        grad_k.astype(jnp.bfloat16).reshape(out_shape),
        grad_v.astype(jnp.bfloat16).reshape(out_shape),
    )


def solution(mesh):
    placed = (
        P("pp", "seq", "tp"),
        P("pp", "seq", "tp"),
        P("pp", "seq", "tp"),
        P("pp", "seq", "tp"),
        P("pp", "tp", None),
        P("pp", "tp"),
        P("pp", "tp", "seq"),
    )
    return jax.shard_map(
        local,
        mesh=mesh,
        in_specs=placed,
        out_specs=(P("pp", "seq", "tp"), P("pp", "seq", "tp"), P("pp", "seq", "tp")),
        check_vma=False,
    )
```

profile of v0, /device:TPU:0, one launch (start us, length us, event | category | flops | bytes accessed | tf_op | source)
XLA Modules:
  0.0 252.6 jit_solution(14396904647753906185)
XLA Ops:
  9.7 3.9 %copy.83 = bf16[1,512,2048]{1,2,0:T(8,128)(2,1)} copy(bf16[1,512,2048]{2,1,0:T(8,128)(2,1)} %param.10) | data formatting | bytes 4194304 | tf_op args[1]
  13.7 2.3 copy.114
  16.0 2.2 fusion.22
  18.3 3.0 %collective-permute-start = (bf16[1,512,1536]{2,1,0:T(8,128)(2,1)}, bf16[1,512,1536]{2,1,0:T(8,128)(2,1)}, u32[]{:S(2)}, u32[]{:S(2)}) collective-permute-start(bf16[1,512,1536]{2,1,0:T(8,128)(2,1)} %param.12), channel_id=1, source_target_pairs={{0,1},{1,0},{2,3},{3,2},{4,5},{5,4},{6,7},{7,6},{8,9},{9,8},{10,11... | collective-permute-start | bytes 4718600 | tf_op jit(solution)/shard_map/ppermute | solution.py:15
  21.4 34.6 %collective-permute-done = bf16[1,512,1536]{2,1,0:T(8,128)(2,1)} collective-permute-done((bf16[1,512,1536]{2,1,0:T(8,128)(2,1)}, bf16[1,512,1536]{2,1,0:T(8,128)(2,1)}, u32[]{:S(2)}, u32[]{:S(2)}) %collective-permute-start) | collective-permute-done | bytes 1572896 | tf_op jit(solution)/shard_map/ppermute | solution.py:15
  57.7 23.2 %all-reduce = f32[128]{0:T(128)S(1)} all-reduce(f32[128]{0:T(128)S(1)} %dynamic-update-slice), channel_id=2, replica_groups=mesh['seq'=8,'tp'=2,'pp'=2] {'seq'}, use_global_device_ids=true, to_apply=%add | all-reduce | flops 128 | bytes 1024
  81.0 4.0 %copy.82 = bf16[1,512,2048]{1,2,0:T(8,128)(2,1)} copy(bf16[1,512,2048]{2,1,0:T(8,128)(2,1)} %param.9) | data formatting | bytes 4194304 | tf_op args[0]
  85.0 7.4 %multiply_convert_fusion.1 = bf16[16,512,512]{2,1,0:T(8,128)(2,1)S(1)} fusion(bf16[512,16,128]{0,2,1:T(8,128)(2,1)} %bitcast.120, bf16[512,16,128]{0,2,1:T(8,128)(2,1)} %bitcast.116, f32[16,512]{1,0:T(8,128)S(1)} %copy_bitcast_fusion, pred[512,512]{1,0:T(8,128)(4,1)S(1)} %iota_compare_fusion), kind=kOutput, calls=%fused_computation.4 | convolution fusion | flops 1094713344 | bytes 12877824 | tf_op jit(solution)/shard_map/thd,shd->hts/dot_general | solution.py:64
  92.5 3.2 %copy-done = bf16[16,512,512]{2,1,0:T(8,128)(2,1)} copy-done((bf16[16,512,512]{2,1,0:T(8,128)(2,1)}, bf16[16,512,512]{2,1,0:T(8,128)(2,1)S(1)}, u32[]{:S(2)}) %copy-start) | copy-done | bytes 8388632
  95.7 4.9 %fusion.16 = f32[16,512,128]{1,2,0:T(8,128)} fusion(bf16[16,512,512]{2,1,0:T(8,128)(2,1)S(1)} %multiply_convert_fusion.1, bf16[512,16,128]{2,1,0:T(8,128)(2,1)S(1)} %bitcast.113), kind=kOutput, calls=%fused_computation.31 | convolution fusion | flops 1073741824 | bytes 14680064 | tf_op jit(solution)/shard_map/hts,shd->thd/dot_general | solution.py:86
  100.5 3.8 %fusion.3 = bf16[16,128,128]{2,1,0:T(8,128)(2,1)S(1)} fusion(bf16[8,16,128,128]{3,2,1,0:T(8,128)(2,1)} %bitcast.128, f32[8,16]{1,0:T(8,128)S(1)} %exponential_select_fusion.1), kind=kLoop, calls=%fused_computation.9 | loop fusion | flops 6029312 | bytes 4719104 | tf_op jit(solution)/shard_map/reduce_sum | solution.py:84
  104.4 5.2 %multiply_reduce_fusion.1 = (f32[512]{0:T(512)S(1)}, f32[512,16,128]{0,2,1:T(8,128)}) fusion(bf16[16,128,128]{2,1,0:T(8,128)(2,1)S(1)} %fusion.3, bf16[512,16,128]{0,2,1:T(8,128)(2,1)S(1)} %bitcast.122, f32[512,16]{0,1:T(8,128)S(1)} %get-tuple-element.179, f32[16,512,128]{1,2,0:T(8,128)} %fusion.16), kind=kOutput, calls=%fused_computation.24 | convolution fusion | flops 272629248 | bytes 11044864 | tf_op jit(solution)/shard_map/thd,hde->the/dot_general | solution.py:87
  109.6 5.4 %copy.92 = f32[512,2048]{1,0:T(8,128)} copy(f32[512,2048]{0,1:T(8,128)} %bitcast.124) | data formatting | bytes 8388608 | tf_op jit(solution)/shard_map/reshape | solution.py:90
  115.0 14.1 %multiply_reduce_fusion = (f32[512]{0:T(512)S(1)}, f32[512,2048]{1,0:T(8,128)}) fusion(f32[512,2048]{1,0:T(8,128)} %copy.92, f32[2048]{0:T(1024)S(1)} %bitcast.131, bf16[1,2048,3072]{2,1,0:T(8,128)(2,1)} %param.13, bf16[1,512,3072]{2,1,0:T(8,128)(2,1)} %all-gather.11.cloned.1.call-done), kind=kOutput, calls=%fused_computation.23 | convolution fusion | flops 6445596160 | bytes 24127488 | tf_op jit(solution)/shard_map/dot_general | solution.py:95
  129.1 2.7 %all-reduce.1 = (f32[512]{0:T(512)S(1)}, f32[512]{0:T(512)S(1)}) all-reduce(f32[512]{0:T(512)S(1)} %get-tuple-element.182, f32[512]{0:T(512)S(1)} %get-tuple-element.184), channel_id=1, replica_groups=mesh['seq'=8,'tp'=2,'pp'=2] {'tp'}, use_global_device_ids=true, to_apply=%region_7.8 | all-reduce | flops 1024 | bytes 8192 | tf_op jit(solution)/shard_map/psum | solution.py:103
  131.8 5.5 %subtract_convert_fusion = bf16[512,2048]{1,0:T(8,128)(2,1)} fusion(f32[512,2048]{1,0:T(8,128)} %copy.92, f32[512,2048]{1,0:T(8,128)} %get-tuple-element.183, f32[512]{0:T(512)S(1)} %get-tuple-element.181, f32[2048]{0:T(1024)S(1)} %bitcast.132, f32[512]{0:T(512)S(1)} %get-tuple-element.180), kind=kLoop, calls=%fused_computation.22 | loop fusion | flops 5242880 | bytes 10498048 | tf_op jit(solution)/shard_map/convert_element_type | solution.py:106
  137.3 2.9 %copy.112 = bf16[512,2048]{0,1:T(8,128)(2,1)S(1)} copy(bf16[512,2048]{1,0:T(8,128)(2,1)} %subtract_convert_fusion) | data formatting | bytes 4194304 | tf_op jit(solution)/shard_map/reshape | solution.py:107
  140.1 3.1 %fusion.25 = bf16[16,128,128]{2,1,0:T(8,128)(2,1)} fusion(bf16[512,16,128]{0,2,1:T(8,128)(2,1)S(1)} %bitcast.108, bf16[512,16,128]{0,2,1:T(8,128)(2,1)} %bitcast.121, f32[512,16]{0,1:T(8,128)S(1)} %get-tuple-element.179), kind=kOutput, calls=%fused_computation.38 | convolution fusion | flops 271843328 | bytes 4751360 | tf_op jit(solution)/shard_map/thd,the->hde/dot_general | solution.py:111
  143.3 16.6 %all-gather.4 = bf16[8,1,16]{2,1,0:T(2,128)(2,1)S(1)} all-gather(bf16[1,1,16]{2,1,0:T(2,128)(2,1)S(1)} %fusion.31), channel_id=1, replica_groups=mesh['seq'=8,'tp'=2,'pp'=2] {'seq'}, dimensions={0}, use_global_device_ids=true | all-gather | bytes 288 | tf_op jit(solution)/shard_map/all_gather | solution.py:21
  159.9 7.2 %multiply_convert_fusion = bf16[16,512,512]{2,1,0:T(8,128)(2,1)S(1)} fusion(bf16[512,16,128]{0,2,1:T(8,128)(2,1)S(1)} %bitcast.109, f32[16,512]{1,0:T(8,128)S(1)} %copy_bitcast_fusion, pred[512,512]{1,0:T(8,128)(4,1)S(1)} %iota_compare_fusion, bf16[512,16,128]{2,1,0:T(8,128)(2,1)} %bitcast.114), kind=kOutput, calls=%fused_computation.3 | convolution fusion | flops 1094713344 | bytes 12877824 | tf_op jit(solution)/shard_map/thd,shd->hts/dot_general | solution.py:108
  167.1 4.8 %fusion.33 = f32[16,512,128]{1,2,0:T(8,128)} fusion(bf16[16,512,512]{2,1,0:T(8,128)(2,1)S(1)} %multiply_convert_fusion, bf16[512,16,128]{0,2,1:T(8,128)(2,1)S(1)} %bitcast.118), kind=kOutput, calls=%fused_computation.60 | convolution fusion | flops 1073741824 | bytes 14680064 | tf_op jit(solution)/shard_map/hts,shd->thd/dot_general | solution.py:118
  171.9 4.2 %fusion.9 = bf16[512,16,128]{0,2,1:T(8,128)(2,1)} fusion(f32[16,512,128]{1,2,0:T(8,128)} %fusion.33, bf16[512,16,128]{0,2,1:T(8,128)(2,1)S(1)} %bitcast.110, f32[512,16]{0,1:T(8,128)S(1)} %get-tuple-element.179, bf16[16,128,128]{2,1,0:T(8,128)(2,1)S(1)} %copy-done.11), kind=kOutput, calls=%fused_computation.18 | convolution fusion | flops 271581184 | bytes 8945664 | tf_op jit(solution)/shard_map/the,hde->thd/dot_general | solution.py:119
  176.1 3.9 %copy.102 = bf16[1,512,2048]{2,1,0:T(8,128)(2,1)} copy(bf16[1,512,2048]{1,2,0:T(8,128)(2,1)} %bitcast.125) | data formatting | bytes 4194304
  180.0 6.6 %fusion.34 = f32[16,128,512]{2,1,0:T(8,128)} fusion(bf16[512,16,128]{0,2,1:T(8,128)(2,1)S(1)} %bitcast.111, bf16[16,512,512]{2,1,0:T(8,128)(2,1)} %copy-done), kind=kOutput, calls=%fused_computation.61 | convolution fusion | flops 1073741824 | bytes 14680064 | tf_op jit(solution)/shard_map/hts,thd->shd/dot_general | solution.py:126
  186.7 26.9 %all-gather.13.cloned.1.call-done = bf16[128,128,128]{2,1,0:T(8,128)(2,1)} async-done(((bf16[16,128,128]{2,1,0:T(8,128)(2,1)}), bf16[128,128,128]{2,1,0:T(8,128)(2,1)}) %all-gather.13.cloned.1.call-update) | async-done | bytes 4194320 | tf_op jit(solution)/shard_map/all_gather | solution.py:21
  213.5 10.9 %while.16 = (s32[]{:T(128)}, f32[16,128,128]{2,1,0:T(8,128)S(1)}, s32[]{:T(128)}, bf16[8,16]{1,0:T(8,128)(2,1)S(1)}, bf16[8,16,128,128]{3,2,1,0:T(8,128)(2,1)}, ...) while((s32[]{:T(128)}, f32[16,128,128]{2,1,0:T(8,128)S(1)}, s32[]{:T(128)}, ...), condition=%wide.region_9.10_spmd.clone, body=%wide.region_8.9_spmd.clone.sunk | while | flops 1310744 | bytes 2621767 | solution.py:39
  213.6 1.4 fusion.52
  224.4 3.2 %fusion.18 = f32[16,128,512]{2,1,0:T(8,128)} fusion(bf16[512,16,128]{2,1,0:T(8,128)(2,1)S(1)} %bitcast.115, f32[16,128,128]{2,1,0:T(8,128)S(1)} %get-tuple-element.135), kind=kOutput, calls=%fused_computation.33 | convolution fusion | flops 268697600 | bytes 7340032 | tf_op jit(solution)/shard_map/the,hde->thd/dot_general | solution.py:123
  228.8 2.1 fusion.5
  230.9 4.1 %copy.104 = bf16[1,512,2048]{2,1,0:T(8,128)(2,1)} copy(bf16[1,512,2048]{1,2,0:T(8,128)(2,1)} %bitcast.126) | data formatting | bytes 4194304
  235.0 7.2 %fusion.7 = bf16[512,16,128]{0,2,1:T(8,128)(2,1)} fusion(f32[16,128,512]{2,1,0:T(8,128)} %fusion.18, bf16[512,16,128]{0,2,1:T(8,128)(2,1)S(1)} %bitcast.123, bf16[16,512,512]{2,1,0:T(8,128)(2,1)} %copy-done.1, f32[512,16]{0,1:T(8,128)S(1)} %get-tuple-element.178), kind=kOutput, calls=%fused_computation.15 | convolution fusion | flops 1076887552 | bytes 16809984 | tf_op jit(solution)/shard_map/hts,thd->shd/dot_general | solution.py:122
  242.2 3.9 %copy.103 = bf16[1,512,2048]{2,1,0:T(8,128)(2,1)} copy(bf16[1,512,2048]{1,2,0:T(8,128)(2,1)} %bitcast.127) | data formatting | bytes 4194304
  (72 shorter events, 14.1 us)
Async XLA Ops:
  7.2 93.4 %all-gather.9.cloned.1.call-start = ((), (), s32[]{:S(2)}) async-start(), calls=%async_computation | async-start | bytes 4718592 | tf_op jit(solution)/shard_map/all_gather | solution.py:77
  13.6 2.4 copy-start.5
  16.0 76.4 %copy-start.3 = (bf16[64,8,16,128]{3,2,1,0:T(8,128)(2,1)}, bf16[64,8,16,128]{3,2,1,0:T(8,128)(2,1)S(1)}, u32[]{:S(2)}) copy-start(bf16[64,8,16,128]{3,2,1,0:T(8,128)(2,1)S(1)} %copy.114) | copy-start | bytes 6291460
  16.0 40.1 %copy-start.13 = (u32[32]{0:T(128)S(1)}, u32[32]{0:T(128)}, u32[]{:S(2)}) copy-start(u32[32]{0:T(128)} %constant.80) | copy-start | bytes 388
  18.3 96.8 %all-gather.11.cloned.1.call-start = ((), (), s32[]{:S(2)}) async-start(), calls=%async_computation.1 | async-start | bytes 4718592 | tf_op jit(solution)/shard_map/all_gather | solution.py:96
  18.3 37.7 %collective-permute-start = (bf16[1,512,1536]{2,1,0:T(8,128)(2,1)}, bf16[1,512,1536]{2,1,0:T(8,128)(2,1)}, u32[]{:S(2)}, u32[]{:S(2)}) collective-permute-start(bf16[1,512,1536]{2,1,0:T(8,128)(2,1)} %param.12), channel_id=1, source_target_pairs={{0,1},{1,0},{2,3},{3,2},{4,5},{5,4},{6,7},{7,6},{8,9},{9,8},{10,11... | collective-permute-start | bytes 4718600 | tf_op jit(solution)/shard_map/ppermute | solution.py:15
  56.1 157.5 %all-gather.13.cloned.1.call-start = ((), (), s32[]{:S(2)}) async-start(), calls=%async_computation.2 | async-start | bytes 4718592 | tf_op jit(solution)/shard_map/all_gather | solution.py:21
  92.5 3.2 %copy-start = (bf16[16,512,512]{2,1,0:T(8,128)(2,1)}, bf16[16,512,512]{2,1,0:T(8,128)(2,1)S(1)}, u32[]{:S(2)}) copy-start(bf16[16,512,512]{2,1,0:T(8,128)(2,1)S(1)} %multiply_convert_fusion.1) | copy-start | bytes 25165828
  100.5 3.8 %copy-start.8 = (bf16[1,512,2048]{1,2,0:T(8,128)(2,1)S(1)}, bf16[1,512,2048]{1,2,0:T(8,128)(2,1)}, u32[]{:S(2)}) copy-start(bf16[1,512,2048]{1,2,0:T(8,128)(2,1)} %copy.82) | copy-start | bytes 6291460
  104.3 5.3 %copy-start.10 = (bf16[16,128,128]{2,1,0:T(8,128)(2,1)}, bf16[16,128,128]{2,1,0:T(8,128)(2,1)S(1)}, u32[]{:S(2)}) copy-start(bf16[16,128,128]{2,1,0:T(8,128)(2,1)S(1)} %fusion.3) | copy-start | bytes 1572868
  109.6 5.4 %copy-start.12 = (f32[1,2048]{1,0:T(1,128)S(1)}, f32[1,2048]{1,0:T(1,128)}, u32[]{:S(2)}) copy-start(f32[1,2048]{1,0:T(1,128)} %param.14) | copy-start | bytes 24580
  159.9 7.2 %copy-start.6 = (bf16[1,512,2048]{1,2,0:T(8,128)(2,1)S(1)}, bf16[1,512,2048]{1,2,0:T(8,128)(2,1)}, u32[]{:S(2)}) copy-start(bf16[1,512,2048]{1,2,0:T(8,128)(2,1)} %copy.83) | copy-start | bytes 6291460
  167.1 4.8 %copy-start.1 = (bf16[16,512,512]{2,1,0:T(8,128)(2,1)}, bf16[16,512,512]{2,1,0:T(8,128)(2,1)S(1)}, u32[]{:S(2)}) copy-start(bf16[16,512,512]{2,1,0:T(8,128)(2,1)S(1)} %multiply_convert_fusion) | copy-start | bytes 25165828
  167.1 4.8 %copy-start.11 = (bf16[16,128,128]{2,1,0:T(8,128)(2,1)S(1)}, bf16[16,128,128]{2,1,0:T(8,128)(2,1)}, u32[]{:S(2)}) copy-start(bf16[16,128,128]{2,1,0:T(8,128)(2,1)} %copy-done.10) | copy-start | bytes 1572868
  213.5 10.9 %copy-start.4 = (bf16[64,8,16,128]{3,2,1,0:T(8,128)(2,1)S(1)}, bf16[64,8,16,128]{3,2,1,0:T(8,128)(2,1)}, u32[]{:S(2)}) copy-start(bf16[64,8,16,128]{3,2,1,0:T(8,128)(2,1)} %copy-done.3) | copy-start | bytes 6291460
  224.4 3.2 %copy-start.2 = (f32[16,128,512]{2,1,0:T(8,128)S(1)}, f32[16,128,512]{2,1,0:T(8,128)}, u32[]{:S(2)}) copy-start(f32[16,128,512]{2,1,0:T(8,128)} %fusion.34) | copy-start | bytes 12582916
  224.4 4.4 %copy-start.7 = (bf16[1,512,2048]{1,2,0:T(8,128)(2,1)S(1)}, bf16[1,512,2048]{1,2,0:T(8,128)(2,1)}, u32[]{:S(2)}) copy-start(bf16[1,512,2048]{1,2,0:T(8,128)(2,1)} %copy.83) | copy-start | bytes 6291460
  230.9 4.1 %copy-start.9 = (bf16[1,512,2048]{1,2,0:T(8,128)(2,1)S(1)}, bf16[1,512,2048]{1,2,0:T(8,128)(2,1)}, u32[]{:S(2)}) copy-start(bf16[1,512,2048]{1,2,0:T(8,128)(2,1)} %copy.82) | copy-start | bytes 6291460
Sparse Core Ops, SparseCore 0:
  18.4 76.1 all-gather.8
  96.1 10.6 all-gather.10
  143.4 70.0 all-gather.12
where the time goes:
time: 254 us; the launch traced here: 253 us
  matrix products  72.3 us (28%)
  waiting for transfers between devices  61.6 us (24%)
  blocking collectives  42.4 us (17%)
  local copies, waits for them, and re-layouts  36.8 us (14%)
  other arithmetic  21.4 us (8%)
  between operations  14.6 us (6%)
  starting transfers between devices  3.16 us (1%)
    ppermute x1, waiting for transfers between devices, from_behind(): return lax.ppermute(value, axis, pairs)  34.6 us
    unnamed x38, local copies, waits for them, and re-layouts  27.3 us
    all_gather x1, waiting for transfers between devices, carried_in(): lax.all_gather(part.astype(kind), axis)  26.9 us
    unnamed x1, blocking collectives  23.2 us
    all_gather x1, blocking collectives, carried_in(): lax.all_gather(part.astype(kind), axis)  16.6 us
    dot_general x1, matrix products, local(): lax.dot_general(lax.all_gather(received[0], 'tp', axis=1, tiled=True), we...  14.1 us
    select_n x8, other arithmetic, lap(): return jax.tree.map(lambda a, b: jnp.where(reached, a, b), new, before)  10.5 us
    dot_general x1, matrix products, local(): jnp.einsum('thd,shd->hts', query_rows, key_rows, preferred_element_type=j...  7.43 us
  transfers between devices with their start and end apart: 4, of which 2 were waited for; matrix products, arithmetic and copies ran while one was open for 23% of the time, Pallas kernels for 0%

commit v1 on v0

v1 whole, which is shorter than its diff:
```python
import functools

import jax
import jax.numpy as jnp
from jax import lax
from jax.experimental import pallas as pl
from jax.experimental.pallas import tpu as pltpu
from jax.sharding import PartitionSpec as P

HEAD = 128
EPS = 1e-06
HB = 2
ROWS = 256
EXTRA = 16
CHUNKS = 2
F32, BF16 = jnp.float32, jnp.bfloat16
NT = (((1,), (1,)), ((), ()))
TN = (((0,), (0,)), ((), ()))
NN = (((1,), (0,)), ((), ()))


def dot(a, b, dims):
    return lax.dot_general(a, b, dims, preferred_element_type=F32)


def cols(hh):
    return slice(hh * HEAD, (hh + 1) * HEAD)


def decay_rows(cum_ref, hh):
    row = cum_ref[pl.ds(pl.program_id(0) * HB + hh, 1), :]
    return row, jnp.transpose(jnp.broadcast_to(row, (HEAD, row.shape[1])))


def strip_decay(row, column, i):
    width = (i + 1) * ROWS
    part = column[i * ROWS:width]
    spread = jnp.concatenate([part] * (width // HEAD), axis=1) - row[:, :width]
    rows = lax.broadcasted_iota(jnp.int32, (ROWS, width), 0) + i * ROWS
    causal = rows >= lax.broadcasted_iota(jnp.int32, (ROWS, width), 1)
    return jnp.exp(jnp.where(causal, spread, -1e30))


def state_kernel(k_ref, v_ref, cum_ref, out_ref):
    for hh in range(HB):
        _, column = decay_rows(cum_ref, hh)
        total = column[-1:]
        weighted = (k_ref[:, cols(hh)].astype(F32) * jnp.exp(total - column)).astype(BF16)
        out_ref[hh, :HEAD, :] = dot(weighted, v_ref[:, cols(hh)], TN).astype(BF16)
        high = total.astype(BF16).astype(F32)
        mid = (total - high).astype(BF16).astype(F32)
        low = total - high - mid
        place = lax.broadcasted_iota(jnp.int32, (EXTRA, HEAD), 0)
        pieces = jnp.where(place == 0, high, jnp.where(place == 1, mid, low))
        out_ref[hh, HEAD:, :] = jnp.where(place < 3, pieces, 0.0).astype(BF16)


def intra_kernel(q_ref, k_ref, v_ref, cum_ref, out_ref):
    for hh in range(HB):
        row, column = decay_rows(cum_ref, hh)
        for i in range(q_ref.shape[0] // ROWS):
            here, width = slice(i * ROWS, (i + 1) * ROWS), (i + 1) * ROWS
            scores = dot(q_ref[here, cols(hh)], k_ref[:width, cols(hh)], NT)
            masked = (scores * strip_decay(row, column, i)).astype(BF16)
            out_ref[here, cols(hh)] = dot(masked, v_ref[:width, cols(hh)], NN)


def gathered(weight_ref, pieces_ref, hh):
    head = pl.program_id(0) * HB + hh
    total = weight_ref[head, 0] * pieces_ref[0, hh, :HEAD, :].astype(F32)
    for j in range(1, pieces_ref.shape[0]):
        total += weight_ref[head, j] * pieces_ref[j, hh, :HEAD, :].astype(F32)
    return total.astype(BF16)


def inter_kernel(weight_ref, q_ref, intra_ref, cum_ref, pieces_ref, out_ref, state_ref, square_ref):
    @pl.when(pl.program_id(0) == 0)
    def _():
        square_ref[...] = jnp.zeros_like(square_ref)

    for hh in range(HB):
        _, column = decay_rows(cum_ref, hh)
        state = gathered(weight_ref, pieces_ref, hh)
        state_ref[hh] = state
        attended = intra_ref[:, cols(hh)] + jnp.exp(column) * dot(q_ref[:, cols(hh)], state, NN)
        out_ref[:, cols(hh)] = attended
        square_ref[...] += attended * attended


def project_kernel(count, last, *refs):
    refs = refs[1:]
    lefts, rights, rest = refs[:count], refs[count:2 * count], refs[2 * count:]
    total = dot(lefts[0][...], rights[0][...], NT)
    for left, right in zip(lefts[1:], rights[1:]):
        total += dot(left[...], right[...], NT)
    if not last:
        for ref in rest[:-1]:
            total += ref[...]
        rest[-1][...] = total
        return
    *before, attended_ref, gain_ref, out_ref, cross_ref = rest
    for ref in before:
        total += ref[...]
    total = total * gain_ref[...]
    out_ref[...] = total

    @pl.when(pl.program_id(0) == 0)
    def _():
        cross_ref[...] = jnp.zeros_like(cross_ref)

    product = total * attended_ref[...]
    cross = product[:, :HEAD]
    for at in range(HEAD, product.shape[1], HEAD):
        cross += product[:, at:at + HEAD]
    cross_ref[...] += cross


def norm_kernel(norm_ref, att_ref, q_ref, cum_ref, inv_ref, fac_ref, grad_ref, passed_ref):
    for hh in range(HB):
        _, column = decay_rows(cum_ref, hh)
        grad = inv_ref[...] * norm_ref[:, cols(hh)] - fac_ref[...] * att_ref[:, cols(hh)]
        grad = grad.astype(BF16)
        grad_ref[:, cols(hh)] = grad
        weighted = (q_ref[:, cols(hh)].astype(F32) * jnp.exp(column)).astype(BF16)
        passed_ref[hh] = dot(weighted, grad, TN).astype(BF16)


def back_kernel(q_ref, k_ref, v_ref, g_ref, cum_ref, state_ref, gq_ref, gk_ref, gv_ref):
    for hh in range(HB):
        row, column = decay_rows(cum_ref, hh)
        strips = q_ref.shape[0] // ROWS
        for i in reversed(range(strips)):
            here, width = slice(i * ROWS, (i + 1) * ROWS), (i + 1) * ROWS
            decay = strip_decay(row, column, i)
            q, g = q_ref[here, cols(hh)], g_ref[here, cols(hh)]
            k, v = k_ref[:width, cols(hh)], v_ref[:width, cols(hh)]
            masked = (dot(q, k, NT) * decay).astype(BF16)
            dmask = (dot(g, v, NT) * decay).astype(BF16)
            grad_q = dot(dmask, k, NN) + jnp.exp(column[here]) * dot(g, state_ref[hh], NT)
            gq_ref[here, cols(hh)] = grad_q.astype(BF16)
            grad_k, grad_v = dot(dmask, q, TN), dot(masked, g, TN)
            if i == strips - 1:
                gk_ref[:, cols(hh)] = grad_k
                gv_ref[:, cols(hh)] = grad_v
            else:
                gk_ref[:width, cols(hh)] += grad_k
                gv_ref[:width, cols(hh)] += grad_v


def final_kernel(weight_ref, k_ref, v_ref, gk_ref, gv_ref, cum_ref, pieces_ref, ok_ref, ov_ref):
    for hh in range(HB):
        _, column = decay_rows(cum_ref, hh)
        tail = jnp.exp(column[-1:] - column)
        later = gathered(weight_ref, pieces_ref, hh)
        grad_k = gk_ref[:, cols(hh)] + tail * dot(v_ref[:, cols(hh)], later, NT)
        grad_v = gv_ref[:, cols(hh)] + tail * dot(k_ref[:, cols(hh)], later, NN)
        ok_ref[:, cols(hh)] = grad_k.astype(BF16)
        ov_ref[:, cols(hh)] = grad_v.astype(BF16)


def from_behind(value, axis, steps):
    count = lax.axis_size(axis)
    return lax.ppermute(value, axis, [(at, (at + steps) % count) for at in range(count)])


def after(value, *earlier):
    return lax.optimization_barrier((value, *earlier))[0]


def local(queries, keys, values, upstream, out_weight, gain, log_decay):
    tokens, width = queries.shape[1:]
    heads, feats = width // HEAD, upstream.shape[2]
    seq, tp = lax.axis_size("seq"), lax.axis_size("tp")
    features = width * tp
    q, k, v = queries[0], keys[0], values[0]
    shape = jax.ShapeDtypeStruct

    tile = pl.BlockSpec((tokens, HB * HEAD), lambda h: (0, h))
    cum_spec = pl.BlockSpec((heads, tokens), lambda h: (0, 0))
    lanes = pl.BlockSpec((tokens, HEAD), lambda h: (0, 0))
    scalars = pl.BlockSpec(memory_space=pltpu.SMEM)
    flat_f32, flat_bf16 = shape((tokens, width), F32), shape((tokens, width), BF16)
    lane_sum = shape((tokens, HEAD), F32)

    def per_head(*lead, rows=HEAD):
        zeros = (0,) * len(lead)
        return pl.BlockSpec((*lead, HB, rows, HEAD), lambda h: (*zeros, h, 0, 0))

    def call(kernel, name, in_specs, out_specs, out_shape, micros):
        return pl.pallas_call(
            kernel,
            name=name,
            grid=(heads // HB,),
            in_specs=in_specs,
            out_specs=out_specs,
            out_shape=out_shape,
            cost_estimate=pl.CostEstimate(
                flops=int(micros * 9e8), bytes_accessed=int(micros * 1e6), transcendentals=0
            ),
        )

    size = feats // CHUNKS
    received = [
        from_behind(upstream[0, :, at * size:(at + 1) * size], "pp", -1) for at in range(CHUNKS)
    ]

    cum = jnp.cumsum(log_decay[0], axis=1)
    payload = call(
        state_kernel, "states", [tile, tile, cum_spec],
        per_head(rows=HEAD + EXTRA), shape((heads, HEAD + EXTRA, HEAD), BF16), 4,
    )(k, v, cum)
    pieces = lax.all_gather(payload[None], "seq", axis=0, tiled=True)
    intra = call(
        intra_kernel, "intra", [tile, tile, tile, cum_spec], tile, flat_f32, 15,
    )(q, k, v, after(cum, payload))

    totals = jnp.sum(pieces[:, :, HEAD:HEAD + 3, 0].astype(F32), axis=2)
    own = lax.axis_index("seq")
    running = jnp.cumsum(totals, axis=0)
    mine = lax.dynamic_index_in_dim(running, own, 0, keepdims=True)
    before = mine - lax.dynamic_index_in_dim(totals, own, 0, keepdims=True)
    places = jnp.arange(seq, dtype=jnp.int32)[:, None]
    earlier, later = places < own, places > own
    early_weight = jnp.where(earlier, jnp.exp(jnp.where(earlier, before - running, 0.0)), 0.0).T
    gap = running - totals - mine
    late_weight = jnp.where(later, jnp.exp(jnp.where(later, gap, 0.0)), 0.0).T

    attended, state, squares = call(
        inter_kernel, "inter",
        [scalars, tile, tile, cum_spec, per_head(seq, rows=HEAD + EXTRA)],
        [tile, per_head(), lanes], [flat_f32, shape((heads, HEAD, HEAD), BF16), lane_sum], 7,
    )(early_weight, q, intra, cum, pieces)

    me = lax.axis_index("tp")
    owners = jnp.stack([(me + tp - s) % tp for s in range(tp)]).astype(jnp.int32)
    rows = HB * HEAD

    def project(at, total, last):
        parts = [received[at]] + [from_behind(received[at], "tp", s) for s in range(1, tp)]
        left = pl.BlockSpec((tokens, size), lambda n, own: (0, 0))
        block = pl.BlockSpec((tokens, rows), lambda n, own: (0, n))
        sums = pl.BlockSpec((tokens, HEAD), lambda n, own: (0, 0))
        rights = [
            pl.BlockSpec((rows, size), functools.partial(
                lambda s, n, own: (n, own[s] * CHUNKS + at), s))
            for s in range(tp)
        ]
        extra = [] if total is None else [total]
        extra_specs = [block] * len(extra)
        if last:
            extra += [attended, gain]
            extra_specs += [block, pl.BlockSpec((1, rows), lambda n, own: (0, n))]
        return pl.pallas_call(
            functools.partial(project_kernel, tp, last),
            name="project",
            grid_spec=pltpu.PrefetchScalarGridSpec(
                num_scalar_prefetch=1,
                grid=(width // rows,),
                in_specs=[left] * tp + rights + extra_specs,
                out_specs=[block, sums] if last else block,
            ),
            out_shape=[flat_f32, lane_sum] if last else flat_f32,
            cost_estimate=pl.CostEstimate(
                flops=2 * tokens * width * size * tp,
                bytes_accessed=2 * size * tp * width + 4 * tokens * width,
                transcendentals=0,
            ),
        )(owners, *parts, *[out_weight[0]] * tp, *extra)

    total = None
    for at in range(CHUNKS):
        received[at] = after(received[at], intra if total is None else total)
        total = project(at, total, at == CHUNKS - 1)
    grad_norm, crosses = total

    sums = lax.psum(jnp.stack([jnp.sum(squares, axis=1), jnp.sum(crosses, axis=1)]), "tp")
    inverse = 1.0 / jnp.sqrt(sums[0] / features + EPS)
    factor = inverse * inverse * inverse * (sums[1] / features)
    inverse = jnp.broadcast_to(inverse[:, None], (tokens, HEAD))
    factor = jnp.broadcast_to(factor[:, None], (tokens, HEAD))
    grad_attn, passed = call(
        norm_kernel, "norm", [tile, tile, tile, cum_spec, lanes, lanes],
        [tile, per_head()], [flat_bf16, shape((heads, HEAD, HEAD), BF16)], 5,
    )(grad_norm, attended, q, cum, inverse, factor)
    passes = lax.all_gather(passed[None], "seq", axis=0, tiled=True)
    grad_q, part_k, part_v = call(
        back_kernel, "back", [tile] * 4 + [cum_spec, per_head()],
        [tile] * 3, [flat_bf16, flat_f32, flat_f32], 25,
    )(q, k, v, grad_attn, after(cum, passed), state)
    grad_k, grad_v = call(
        final_kernel, "final", [scalars] + [tile] * 4 + [cum_spec, per_head(seq)],
        [tile] * 2, [flat_bf16, flat_bf16], 7,
    )(late_weight, k, v, part_k, part_v, cum, passes)
    return grad_q[None], grad_k[None], grad_v[None]


def solution(mesh):
    placed = (
        P("pp", "seq", "tp"),
        P("pp", "seq", "tp"),
        P("pp", "seq", "tp"),
        P("pp", "seq", "tp"),
        P("pp", "tp", None),
        P("pp", "tp"),
        P("pp", "tp", "seq"),
    )
    return jax.shard_map(
        local,
        mesh=mesh,
        in_specs=placed,
        out_specs=(P("pp", "seq", "tp"), P("pp", "seq", "tp"), P("pp", "seq", "tp")),
        check_vma=False,
    )
```

time: 254 us -> 230 us (0.906)
  Pallas kernels: 0 us -> 85.9 us
  matrix products: 72.3 us -> 0 us
  waiting for transfers between devices: 61.6 us -> 110 us
  blocking collectives: 42.4 us -> 2.47 us
  local copies, waits for them, and re-layouts: 36.8 us -> 4.52 us
  other arithmetic: 21.4 us -> 7 us
    pallas_call x0 -> x8, Pallas kernels: none -> 85.9 us  [the longest x2 22.7 us: project(): pl.pallas_call(functools.partial(project_kernel, tp, last), name='project...]
    dot_general x13 -> x0, matrix products: 72.3 us -> none  [the longest x1 14.1 us: local(): lax.dot_general(lax.all_gather(received[0], 'tp', axis=1, tiled=True), we...]
    all_gather x3 -> x2, waiting for transfers between devices: 26.9 us -> 96.6 us  [the longest x1 55.1 us: local(): passes = lax.all_gather(passed[None], 'seq', axis=0, tiled=True)]
    unnamed x38 -> x10, local copies, waits for them, and re-layouts: 27.3 us -> 1.75 us
    unnamed x1 -> x0, blocking collectives: 23.2 us -> none
    ppermute x1 -> x4, waiting for transfers between devices: 34.6 us -> 13.1 us  [from_behind(): lax.ppermute(value, axis, [(at, (at + steps) % count) for at in range(cou...]
    all_gather x1 -> x0, blocking collectives: 16.6 us -> none  [carried_in(): lax.all_gather(part.astype(kind), axis)]
    select_n x9 -> x1, other arithmetic: 10.6 us -> 0.69 us  [local(): late_weight = jnp.where(later, jnp.exp(jnp.where(later, gap, 0.0)), 0.0).T]
  transfers between devices with their start and end apart: 4 -> 6, of which waited for: 2 -> 4; matrix products, arithmetic and copies ran while one was open for 23% -> 2% of each run, Pallas kernels for 0% -> 20%
where the time goes in v1:
time: 230 us; the launch traced here: 229 us
  waiting for transfers between devices  110 us (48%)
  Pallas kernels  85.9 us (37%)
  between operations  14.1 us (6%)
  other arithmetic  7 us (3%)
  starting transfers between devices  4.85 us (2%)
  local copies, waits for them, and re-layouts  4.52 us (2%)
  blocking collectives  2.47 us (1%)
    all_gather x1, waiting for transfers between devices, local(): passes = lax.all_gather(passed[None], 'seq', axis=0, tiled=True)  55.1 us
    all_gather x1, waiting for transfers between devices, local(): pieces = lax.all_gather(payload[None], 'seq', axis=0, tiled=True)  41.5 us
    pallas_call x2, Pallas kernels, project(): pl.pallas_call(functools.partial(project_kernel, tp, last), name='project...  22.7 us
    pallas_call x1, Pallas kernels, local(): call(back_kernel, 'back', [tile] * 4 + [cum_spec, per_head()], [tile] * 3...  16.2 us
    ppermute x4, waiting for transfers between devices, from_behind(): lax.ppermute(value, axis, [(at, (at + steps) % count) for at in range(cou...  13.1 us
    pallas_call x1, Pallas kernels, local(): call(intra_kernel, 'intra', [tile, tile, tile, cum_spec], tile, flat_f32,...  10.8 us
    pallas_call x1, Pallas kernels, local(): call(final_kernel, 'final', [scalars] + [tile] * 4 + [cum_spec, per_head(...  10.5 us
    pallas_call x1, Pallas kernels, local(): call(inter_kernel, 'inter', [scalars, tile, tile, cum_spec, per_head(seq,...  9.3 us
  transfers between devices with their start and end apart: 6, of which 4 were waited for; matrix products, arithmetic and copies ran while one was open for 2% of the time, Pallas kernels for 20%

profile of v1, /device:TPU:0, one launch (start us, length us, event | category | flops | bytes accessed | tf_op | source)
XLA Modules:
  0.0 228.6 jit_solution(5963447684617452928)
XLA Ops:
  7.2 0.8 reshape.53
  8.0 1.2 reduce-window.6
  9.1 0.2 slice_reduce_fusion
  9.3 0.7 copy_bitcast_fusion.cum_ref
  10.0 7.5 %states.1 = bf16[16,144,128]{2,1,0:T(8,128)(2,1)} custom-call(bf16[512,2048]{1,0:T(8,128)(2,1)} %bitcast.44, bf16[512,2048]{1,0:T(8,128)(2,1)} %bitcast.48, f32[16,512]{1,0:T(8,128)} %copy_bitcast_fusion.cum_ref), custom_call_target="tpu_custom_call" | custom-call | flops 3600000000 | bytes 4000000 | tf_op jit(solution)/shard_map/states/pallas_call | solution.py:208
  17.6 0.1 slice_bitcast_fusion
  17.7 3.0 %collective-permute-start.1 = (bf16[512,768]{1,0:T(8,128)(2,1)S(1)}, bf16[512,768]{1,0:T(8,128)(2,1)S(1)}, u32[]{:S(2)}, u32[]{:S(2)}) collective-permute-start(bf16[512,768]{1,0:T(8,128)(2,1)S(1)} %get-tuple-element.37), channel_id=1, source_target_pairs={{0,1},{1,0},{2,3},{3,2},{4,5},{5,4},{6,7},{7,6},{8,9},{9,8},{10,11... | collective-permute-start | bytes 2359304 | tf_op jit(solution)/shard_map/ppermute | solution.py:163
  20.8 10.8 %intra.1.intra_ref = f32[512,2048]{1,0:T(8,128)} custom-call(bf16[512,2048]{1,0:T(8,128)(2,1)} %bitcast.40, bf16[512,2048]{1,0:T(8,128)(2,1)} %bitcast.45, bf16[512,2048]{1,0:T(8,128)(2,1)} %bitcast.49, f32[16,512]{1,0:T(8,128)} %copy_bitcast_fusion.cum_ref), custom_call_target="tpu_custom_call" | custom-call | flops 13500000256 | bytes 15000000 | tf_op jit(solution)/shard_map/intra/pallas_call | solution.py:213
  31.6 6.7 %collective-permute-done.1.refs_1_ = bf16[512,768]{1,0:T(8,128)(2,1)S(1)} collective-permute-done((bf16[512,768]{1,0:T(8,128)(2,1)S(1)}, bf16[512,768]{1,0:T(8,128)(2,1)S(1)}, u32[]{:S(2)}, u32[]{:S(2)}) %collective-permute-start.1) | collective-permute-done | bytes 786464 | tf_op jit(solution)/shard_map/ppermute | solution.py:163
  38.3 1.7 collective-permute-start
  40.1 0.6 pad_add_fusion.refs_0_
  40.7 0.9 copy-done.2
  41.6 10.3 %project.2.refs_5_ = f32[512,2048]{1,0:T(8,128)} custom-call(s32[2]{0:T(128)} %pad_add_fusion.refs_0_, bf16[512,768]{1,0:T(8,128)(2,1)} %copy-done.1, bf16[512,768]{1,0:T(8,128)(2,1)} %copy-done.2, bf16[2048,3072]{1,0:T(8,128)(2,1)} %bitcast.28, bf16[2048,3072]{1,0:T(8,128)(2,1)} %bitcast.29), custom_call_target="tpu_custom_call" | custom-call | flops 3221225472 | bytes 10485760 | tf_op jit(solution)/shard_map/project/pallas_call | solution.py:253
  51.9 6.4 %collective-permute-done.refs_1_ = bf16[512,768]{1,0:T(8,128)(2,1)S(1)} collective-permute-done((bf16[512,768]{1,0:T(8,128)(2,1)S(1)}, bf16[512,768]{1,0:T(8,128)(2,1)S(1)}, u32[]{:S(2)}, u32[]{:S(2)}) %collective-permute-start) | collective-permute-done | bytes 786464 | tf_op jit(solution)/shard_map/ppermute | solution.py:163
  58.3 41.5 %all-gather.5.cloned.1.call-done = bf16[128,144,128]{2,1,0:T(8,128)(2,1)} async-done(((bf16[16,144,128]{2,1,0:T(8,128)(2,1)}), bf16[128,144,128]{2,1,0:T(8,128)(2,1)}) %all-gather.5.cloned.1.call-update) | async-done | bytes 4718608 | tf_op jit(solution)/shard_map/all_gather | solution.py:212
  99.8 1.2 convert_reduce_fusion
  101.0 0.1 copy.16
  101.1 0.2 reduce_window_sum.28
  101.3 0.2 dynamic-slice_reduce_fusion
  101.5 0.7 select_bitcast_fusion
  102.2 9.3 %inter.1 = (f32[512,2048]{1,0:T(8,128)}, bf16[16,128,128]{2,1,0:T(8,128)(2,1)}, f32[512,128]{1,0:T(8,128)}) custom-call(f32[16,8]{1,0:T(8,128)} %get-tuple-element.40.weight_ref, bf16[512,2048]{1,0:T(8,128)(2,1)} %bitcast.41, f32[512,2048]{1,0:T(8,128)} %intra.1.intra_ref, f32[16,512]{1,0:T(8,128)} %copy_bitcast_fusion.cum_ref, ...), custom_call_target="tpu_custom_call" | custom-call | flops 6300000256 | bytes 7000000 | tf_op jit(solution)/shard_map/inter/pallas_call | solution.py:228
  111.5 1.1 reduce_sum.28
  112.6 0.9 copy-done.4
  113.5 12.4 %project.3 = (f32[512,2048]{1,0:T(8,128)}, f32[512,128]{1,0:T(8,128)}) custom-call(s32[2]{0:T(128)} %pad_add_fusion.refs_0_, bf16[512,768]{1,0:T(8,128)(2,1)} %copy-done.3, bf16[512,768]{1,0:T(8,128)(2,1)} %copy-done.4, bf16[2048,3072]{1,0:T(8,128)(2,1)} %bitcast.30, bf16[2048,3072]{1,0:T(8,128)(2,1)} %bitcast.31, f32[512,2048]{1,0:T(8,128)} %project.2.refs_5_, ...), custom_call_target="tpu_custom_call" | custom-call | flops 3221225472 | bytes 10485760 | tf_op jit(solution)/shard_map/project/pallas_call | solution.py:253
  125.9 1.1 reduce_sum.29
  127.0 2.5 %psum.7 = f32[2,512]{1,0:T(2,128)S(1)} all-reduce(f32[2,512]{1,0:T(2,128)S(1)} %pad_maximum_fusion), channel_id=1, replica_groups=mesh['seq'=8,'tp'=2,'pp'=2] {'tp'}, use_global_device_ids=true, to_apply=%region_6.7 | all-reduce | flops 1024 | bytes 8192 | tf_op jit(solution)/shard_map/psum | solution.py:276
  129.5 0.8 broadcast_in_dim.61.inv_ref
  130.3 0.8 broadcast_in_dim.62.fac_ref
  131.1 8.9 %norm.1 = (bf16[512,2048]{1,0:T(8,128)(2,1)}, bf16[16,128,128]{2,1,0:T(8,128)(2,1)}) custom-call(f32[512,2048]{1,0:T(8,128)} %get-tuple-element.23.norm_ref, f32[512,2048]{1,0:T(8,128)} %get-tuple-element.22.refs_6_.att_ref, bf16[512,2048]{1,0:T(8,128)(2,1)} %bitcast.42, f32[16,512]{1,0:T(8,128)} %copy_bitcast_fusion.cum_ref, ...), custom_call_target="tpu_custom_call" | custom-call | flops 4499999744 | bytes 5000000 | tf_op jit(solution)/shard_map/norm/pallas_call | solution.py:281
  140.0 16.2 %back.1 = (bf16[512,2048]{1,0:T(8,128)(2,1)}, f32[512,2048]{1,0:T(8,128)}, f32[512,2048]{1,0:T(8,128)}) custom-call(bf16[512,2048]{1,0:T(8,128)(2,1)} %bitcast.43, bf16[512,2048]{1,0:T(8,128)(2,1)} %bitcast.46, bf16[512,2048]{1,0:T(8,128)(2,1)} %bitcast.50, bf16[512,2048]{1,0:T(8,128)(2,1)} %get-tuple-element.26.g_ref, f32[16,512]{1,0:T(8,128)} %copy_bitcast_fusion.cum_ref, ...), custom_call_target="tpu_custom_call" | custom-call | flops 22499999744 | bytes 25000000 | tf_op jit(solution)/shard_map/back/pallas_call | solution.py:286
  156.2 55.1 %all-gather.7.cloned.1.call-done = bf16[128,128,128]{2,1,0:T(8,128)(2,1)} async-done(((bf16[16,128,128]{2,1,0:T(8,128)(2,1)}), bf16[128,128,128]{2,1,0:T(8,128)(2,1)}) %all-gather.7.cloned.1.call-update) | async-done | bytes 4194320 | tf_op jit(solution)/shard_map/all_gather | solution.py:285
  211.3 10.5 %final.1 = (bf16[512,2048]{1,0:T(8,128)(2,1)}, bf16[512,2048]{1,0:T(8,128)(2,1)}) custom-call(f32[16,8]{1,0:T(8,128)} %get-tuple-element.39.weight_ref, bf16[512,2048]{1,0:T(8,128)(2,1)} %bitcast.47, bf16[512,2048]{1,0:T(8,128)(2,1)} %bitcast.51, f32[512,2048]{1,0:T(8,128)} %get-tuple-element.31.gk_ref, f32[512,2048]{1,0:T(8,128)} %get-tuple-element.32.gv_ref, ...), custom_call_target="tpu_custom_call" | custom-call | flops 6300000256 | bytes 7000000 | tf_op jit(solution)/shard_map/final/pallas_call | solution.py:290
  (23 shorter events, 0.2 us)
Async XLA Ops:
  7.2 92.6 %all-gather.5.cloned.1.call-start = ((), (), s32[]{:S(2)}) async-start(), calls=%async_computation | async-start | bytes 5308416 | tf_op jit(solution)/shard_map/all_gather | solution.py:212
  10.0 7.6 %copy-start = (bf16[1,512,1536]{2,1,0:T(8,128)(2,1)S(1)}, bf16[1,512,1536]{2,1,0:T(8,128)(2,1)}, u32[]{:S(2)}) copy-start(bf16[1,512,1536]{2,1,0:T(8,128)(2,1)} %param.10) | copy-start | bytes 4718596
  17.6 193.8 %all-gather.7.cloned.1.call-start = ((), (), s32[]{:S(2)}) async-start(), calls=%async_computation.1 | async-start | bytes 4718592 | tf_op jit(solution)/shard_map/all_gather | solution.py:285
  17.7 20.6 %collective-permute-start.1 = (bf16[512,768]{1,0:T(8,128)(2,1)S(1)}, bf16[512,768]{1,0:T(8,128)(2,1)S(1)}, u32[]{:S(2)}, u32[]{:S(2)}) collective-permute-start(bf16[512,768]{1,0:T(8,128)(2,1)S(1)} %get-tuple-element.37), channel_id=1, source_target_pairs={{0,1},{1,0},{2,3},{3,2},{4,5},{5,4},{6,7},{7,6},{8,9},{9,8},{10,11... | collective-permute-start | bytes 2359304 | tf_op jit(solution)/shard_map/ppermute | solution.py:163
  38.3 2.4 %copy-start.1 = (bf16[512,768]{1,0:T(8,128)(2,1)}, bf16[512,768]{1,0:T(8,128)(2,1)S(1)}, u32[]{:S(2)}) copy-start(bf16[512,768]{1,0:T(8,128)(2,1)S(1)} %collective-permute-done.1.refs_1_) | copy-start | bytes 2359300
  38.3 2.4 %collective-permute-start.2 = (bf16[512,768]{1,0:T(8,128)(2,1)S(1)}, bf16[512,768]{1,0:T(8,128)(2,1)S(1)}, u32[]{:S(2)}, u32[]{:S(2)}) collective-permute-start(bf16[512,768]{1,0:T(8,128)(2,1)S(1)} %collective-permute-done.1.refs_1_), channel_id=1, source_target_pairs={{0,2},{2,0},{1,3},{3,1},{4,6},{6,4},{5,7},{7,5},{8,10},{10,8},{9,1... | collective-permute-start | bytes 2359304 | tf_op jit(solution)/shard_map/ppermute | solution.py:163
  38.3 20.0 %collective-permute-start = (bf16[512,768]{1,0:T(8,128)(2,1)S(1)}, bf16[512,768]{1,0:T(8,128)(2,1)S(1)}, u32[]{:S(2)}, u32[]{:S(2)}) collective-permute-start(bf16[512,768]{1,0:T(8,128)(2,1)S(1)} %get-tuple-element.38), channel_id=1, source_target_pairs={{0,1},{1,0},{2,3},{3,2},{4,5},{5,4},{6,7},{7,6},{8,9},{9,8},{10,11... | collective-permute-start | bytes 2359304 | tf_op jit(solution)/shard_map/ppermute | solution.py:163
  40.7 0.9 copy-start.2
  58.3 53.2 %copy-start.3 = (bf16[512,768]{1,0:T(8,128)(2,1)}, bf16[512,768]{1,0:T(8,128)(2,1)S(1)}, u32[]{:S(2)}) copy-start(bf16[512,768]{1,0:T(8,128)(2,1)S(1)} %collective-permute-done.refs_1_) | copy-start | bytes 2359300
  58.3 54.3 %collective-permute-start.3 = (bf16[512,768]{1,0:T(8,128)(2,1)S(1)}, bf16[512,768]{1,0:T(8,128)(2,1)S(1)}, u32[]{:S(2)}, u32[]{:S(2)}) collective-permute-start(bf16[512,768]{1,0:T(8,128)(2,1)S(1)} %collective-permute-done.refs_1_), channel_id=1, source_target_pairs={{0,2},{2,0},{1,3},{3,1},{4,6},{6,4},{5,7},{7,5},{8,10},{10,8},{9,1... | collective-permute-start | bytes 2359304 | tf_op jit(solution)/shard_map/ppermute | solution.py:163
  112.6 0.9 copy-start.4
Sparse Core Ops, SparseCore 0:
  17.7 82.0 all-gather.4
  140.1 71.1 all-gather.6

commit v2 on v1

--- a/solution.py
+++ b/solution.py
@@ -12,7 +12,7 @@
 HB = 2
 ROWS = 256
 EXTRA = 16
-CHUNKS = 2
+CHUNKS = 1
 F32, BF16 = jnp.float32, jnp.bfloat16
 NT = (((1,), (1,)), ((), ()))
 TN = (((0,), (0,)), ((), ()))
@@ -41,21 +41,111 @@
     return jnp.exp(jnp.where(causal, spread, -1e30))
 
 
+def total_rows(total):
+    high = total.astype(BF16).astype(F32)
+    mid = (total - high).astype(BF16).astype(F32)
+    low = total - high - mid
+    place = lax.broadcasted_iota(jnp.int32, (EXTRA, HEAD), 0)
+    pieces = jnp.where(place == 0, high, jnp.where(place == 1, mid, low))
+    return jnp.where(place < 3, pieces, 0.0).astype(BF16)
+
+
+def store_units(out_ref, hh, state, total):
+    part = out_ref.shape[1] - EXTRA
+    split = HEAD // part
+    for at in range(split):
+        out_ref[hh * split + at, :part, :] = state[at * part:(at + 1) * part]
+        out_ref[hh * split + at, part:, :] = total_rows(total)
+
+
 def state_kernel(k_ref, v_ref, cum_ref, out_ref):
     for hh in range(HB):
         _, column = decay_rows(cum_ref, hh)
         total = column[-1:]
         weighted = (k_ref[:, cols(hh)].astype(F32) * jnp.exp(total - column)).astype(BF16)
-        out_ref[hh, :HEAD, :] = dot(weighted, v_ref[:, cols(hh)], TN).astype(BF16)
-        high = total.astype(BF16).astype(F32)
-        mid = (total - high).astype(BF16).astype(F32)
-        low = total - high - mid
-        place = lax.broadcasted_iota(jnp.int32, (EXTRA, HEAD), 0)
-        pieces = jnp.where(place == 0, high, jnp.where(place == 1, mid, low))
-        out_ref[hh, HEAD:, :] = jnp.where(place < 3, pieces, 0.0).astype(BF16)
-
-
-def intra_kernel(q_ref, k_ref, v_ref, cum_ref, out_ref):
+        store_units(out_ref, hh, dot(weighted, v_ref[:, cols(hh)], TN).astype(BF16), total)
+
+
+def exchange(n, reverse, payload_ref, out_ref, recv, ready, result, send_sem, recv_sem):
+    me, step, steps = lax.axis_index("seq"), pl.program_id(0), pl.num_programs(0)
+    per, part = ready.shape[1:3]
+    split = HEAD // part
+    middle = steps // 2
+
+    def copies(phase, source, target):
+        made = []
+        for off in range(1, n):
+            peer = lax.rem(me + off, n)
+            made.append(pltpu.make_async_remote_copy(
+                src_ref=source(peer),
+                dst_ref=target.at[me],
+                send_sem=send_sem.at[phase, off],
+                recv_sem=recv_sem.at[phase, off],
+                device_id={"seq": peer},
+                device_id_type=pl.DeviceIdType.MESH,
+            ))
+        return made
+
+    def first():
+        return copies(0, lambda peer: payload_ref.at[pl.ds(peer * per, per)], recv)
+
+    def second():
+        return copies(1, lambda peer: ready.at[peer], result)
+
+    def landed(phase, target):
+        for off in range(1, n):
+            peer = lax.rem(me + n - off, n)
+            pltpu.make_async_remote_copy(
+                src_ref=target.at[peer],
+                dst_ref=target.at[peer],
+                send_sem=send_sem.at[phase, off],
+                recv_sem=recv_sem.at[phase, off],
+                device_id={"seq": peer},
+                device_id_type=pl.DeviceIdType.MESH,
+            ).wait_recv()
+
+    @pl.when(step == 0)
+    def _():
+        barrier = pltpu.get_barrier_semaphore()
+        for off in range(1, n):
+            pl.semaphore_signal(
+                barrier, inc=1, device_id={"seq": lax.rem(me + off, n)},
+                device_id_type=pl.DeviceIdType.MESH,
+            )
+        pl.semaphore_wait(barrier, n - 1)
+        for copy in first():
+            copy.start()
+        recv[me] = payload_ref[pl.ds(me * per, per)]
+
+    @pl.when(step == middle)
+    def _():
+        landed(0, recv)
+        for h in range(per):
+            state = jnp.zeros((part, HEAD), F32)
+            for at in reversed(range(n)) if reverse else range(n):
+                ready[at, h] = state.astype(BF16)
+                pieces = recv[at, h, part:, :].astype(F32)
+                total = pieces[0:1] + pieces[1:2] + pieces[2:3]
+                state = jnp.exp(total) * state + recv[at, h, :part, :].astype(F32)
+
+    @pl.when(step == middle + 1)
+    def _():
+        for copy in second():
+            copy.start()
+        result[me] = ready[me]
+
+    @pl.when(step == steps - 1)
+    def _():
+        landed(1, result)
+        for unit in range(n * per):
+            row = unit % split * part
+            out_ref[unit // split, row:row + part, :] = result[unit // per, unit % per]
+        for copy in first() + second():
+            copy.wait_send()
+
+
+def intra_kernel(n, payload_ref, q_ref, k_ref, v_ref, cum_ref, out_ref, state_ref, *scratch):
+    exchange(n, False, payload_ref, state_ref, *scratch)
     for hh in range(HB):
         row, column = decay_rows(cum_ref, hh)
         for i in range(q_ref.shape[0] // ROWS):
@@ -65,24 +155,15 @@
             out_ref[here, cols(hh)] = dot(masked, v_ref[:width, cols(hh)], NN)
 
 
-def gathered(weight_ref, pieces_ref, hh):
-    head = pl.program_id(0) * HB + hh
-    total = weight_ref[head, 0] * pieces_ref[0, hh, :HEAD, :].astype(F32)
-    for j in range(1, pieces_ref.shape[0]):
-        total += weight_ref[head, j] * pieces_ref[j, hh, :HEAD, :].astype(F32)
-    return total.astype(BF16)
-
-
-def inter_kernel(weight_ref, q_ref, intra_ref, cum_ref, pieces_ref, out_ref, state_ref, square_ref):
+def inter_kernel(q_ref, intra_ref, cum_ref, state_ref, out_ref, square_ref):
     @pl.when(pl.program_id(0) == 0)
     def _():
         square_ref[...] = jnp.zeros_like(square_ref)
 
     for hh in range(HB):
         _, column = decay_rows(cum_ref, hh)
-        state = gathered(weight_ref, pieces_ref, hh)
-        state_ref[hh] = state
-        attended = intra_ref[:, cols(hh)] + jnp.exp(column) * dot(q_ref[:, cols(hh)], state, NN)
+        attended = jnp.exp(column) * dot(q_ref[:, cols(hh)], state_ref[hh], NN)
+        attended += intra_ref[:, cols(hh)]
         out_ref[:, cols(hh)] = attended
         square_ref[...] += attended * attended
 
@@ -122,10 +203,14 @@
         grad = grad.astype(BF16)
         grad_ref[:, cols(hh)] = grad
         weighted = (q_ref[:, cols(hh)].astype(F32) * jnp.exp(column)).astype(BF16)
-        passed_ref[hh] = dot(weighted, grad, TN).astype(BF16)
-
-
-def back_kernel(q_ref, k_ref, v_ref, g_ref, cum_ref, state_ref, gq_ref, gk_ref, gv_ref):
+        store_units(passed_ref, hh, dot(weighted, grad, TN).astype(BF16), column[-1:])
+
+
+def back_kernel(
+    n, payload_ref, q_ref, k_ref, v_ref, g_ref, cum_ref, state_ref,
+    gq_ref, gk_ref, gv_ref, later_ref, *scratch,
+):
+    exchange(n, True, payload_ref, later_ref, *scratch)
     for hh in range(HB):
         row, column = decay_rows(cum_ref, hh)
         strips = q_ref.shape[0] // ROWS
@@ -147,11 +232,11 @@
                 gv_ref[:width, cols(hh)] += grad_v
 
 
-def final_kernel(weight_ref, k_ref, v_ref, gk_ref, gv_ref, cum_ref, pieces_ref, ok_ref, ov_ref):
+def final_kernel(k_ref, v_ref, gk_ref, gv_ref, cum_ref, later_ref, ok_ref, ov_ref):
     for hh in range(HB):
         _, column = decay_rows(cum_ref, hh)
         tail = jnp.exp(column[-1:] - column)
-        later = gathered(weight_ref, pieces_ref, hh)
+        later = later_ref[hh]
         grad_k = gk_ref[:, cols(hh)] + tail * dot(v_ref[:, cols(hh)], later, NT)
         grad_v = gv_ref[:, cols(hh)] + tail * dot(k_ref[:, cols(hh)], later, NN)
         ok_ref[:, cols(hh)] = grad_k.astype(BF16)
@@ -178,15 +263,35 @@
     tile = pl.BlockSpec((tokens, HB * HEAD), lambda h: (0, h))
     cum_spec = pl.BlockSpec((heads, tokens), lambda h: (0, 0))
     lanes = pl.BlockSpec((tokens, HEAD), lambda h: (0, 0))
-    scalars = pl.BlockSpec(memory_space=pltpu.SMEM)
     flat_f32, flat_bf16 = shape((tokens, width), F32), shape((tokens, width), BF16)
     lane_sum = shape((tokens, HEAD), F32)
 
-    def per_head(*lead, rows=HEAD):
-        zeros = (0,) * len(lead)
-        return pl.BlockSpec((*lead, HB, rows, HEAD), lambda h: (*zeros, h, 0, 0))
-
-    def call(kernel, name, in_specs, out_specs, out_shape, micros):
+    split = max(1, seq // heads)
+    units, part = heads * split, HEAD // split
+    per, tall = units // seq, part + EXTRA
+    payload_shape = shape((units, tall, HEAD), BF16)
+    payload_tile = pl.BlockSpec((HB * split, tall, HEAD), lambda h: (h, 0, 0))
+    whole_in = pl.BlockSpec((units, tall, HEAD), lambda h: (0, 0, 0))
+    whole_out = pl.BlockSpec((heads, HEAD, HEAD), lambda h: (0, 0, 0))
+    states_bf16 = shape((heads, HEAD, HEAD), BF16)
+
+    per_head = pl.BlockSpec((HB, HEAD, HEAD), lambda h: (h, 0, 0))
+
+    def exchanging(collective):
+        return {
+            "scratch_shapes": [
+                pltpu.VMEM((seq, per, tall, HEAD), BF16),
+                pltpu.VMEM((seq, per, part, HEAD), BF16),
+                pltpu.VMEM((seq, per, part, HEAD), BF16),
+                pltpu.SemaphoreType.DMA((2, seq)),
+                pltpu.SemaphoreType.DMA((2, seq)),
+            ],
+            "compiler_params": pltpu.CompilerParams(
+                collective_id=collective, has_side_effects=True
+            ),
+        }
+
+    def call(kernel, name, in_specs, out_specs, out_shape, micros, **more):
         return pl.pallas_call(
             kernel,
             name=name,
@@ -197,6 +302,7 @@
             cost_estimate=pl.CostEstimate(
                 flops=int(micros * 9e8), bytes_accessed=int(micros * 1e6), transcendentals=0
             ),
+            **more,
         )
 
     size = feats // CHUNKS
@@ -207,29 +313,16 @@
     cum = jnp.cumsum(log_decay[0], axis=1)
     payload = call(
         state_kernel, "states", [tile, tile, cum_spec],
-        per_head(rows=HEAD + EXTRA), shape((heads, HEAD + EXTRA, HEAD), BF16), 4,
+        payload_tile, payload_shape, 7,
     )(k, v, cum)
-    pieces = lax.all_gather(payload[None], "seq", axis=0, tiled=True)
-    intra = call(
-        intra_kernel, "intra", [tile, tile, tile, cum_spec], tile, flat_f32, 15,
-    )(q, k, v, after(cum, payload))
-
-    totals = jnp.sum(pieces[:, :, HEAD:HEAD + 3, 0].astype(F32), axis=2)
-    own = lax.axis_index("seq")
-    running = jnp.cumsum(totals, axis=0)
-    mine = lax.dynamic_index_in_dim(running, own, 0, keepdims=True)
-    before = mine - lax.dynamic_index_in_dim(totals, own, 0, keepdims=True)
-    places = jnp.arange(seq, dtype=jnp.int32)[:, None]
-    earlier, later = places < own, places > own
-    early_weight = jnp.where(earlier, jnp.exp(jnp.where(earlier, before - running, 0.0)), 0.0).T
-    gap = running - totals - mine
-    late_weight = jnp.where(later, jnp.exp(jnp.where(later, gap, 0.0)), 0.0).T
-
-    attended, state, squares = call(
-        inter_kernel, "inter",
-        [scalars, tile, tile, cum_spec, per_head(seq, rows=HEAD + EXTRA)],
-        [tile, per_head(), lanes], [flat_f32, shape((heads, HEAD, HEAD), BF16), lane_sum], 7,
-    )(early_weight, q, intra, cum, pieces)
+    intra, state = call(
+        functools.partial(intra_kernel, seq), "intra", [whole_in, tile, tile, tile, cum_spec],
+        [tile, whole_out], [flat_f32, states_bf16], 30, **exchanging(0),
+    )(payload, q, k, v, cum)
+    attended, squares = call(
+        inter_kernel, "inter", [tile, tile, cum_spec, per_head],
+        [tile, lanes], [flat_f32, lane_sum], 9,
+    )(q, intra, cum, state)
 
     me = lax.axis_index("tp")
     owners = jnp.stack([(me + tp - s) % tp for s in range(tp)]).astype(jnp.int32)
@@ -280,17 +373,16 @@
     factor = jnp.broadcast_to(factor[:, None], (tokens, HEAD))
     grad_attn, passed = call(
         norm_kernel, "norm", [tile, tile, tile, cum_spec, lanes, lanes],
-        [tile, per_head()], [flat_bf16, shape((heads, HEAD, HEAD), BF16)], 5,
+        [tile, payload_tile], [flat_bf16, payload_shape], 9,
     )(grad_norm, attended, q, cum, inverse, factor)
-    passes = lax.all_gather(passed[None], "seq", axis=0, tiled=True)
-    grad_q, part_k, part_v = call(
-        back_kernel, "back", [tile] * 4 + [cum_spec, per_head()],
-        [tile] * 3, [flat_bf16, flat_f32, flat_f32], 25,
-    )(q, k, v, grad_attn, after(cum, passed), state)
+    grad_q, part_k, part_v, later = call(
+        functools.partial(back_kernel, seq), "back", [whole_in] + [tile] * 4 + [cum_spec, per_head],
+        [tile] * 3 + [whole_out], [flat_bf16, flat_f32, flat_f32, states_bf16], 30, **exchanging(1),
+    )(passed, q, k, v, grad_attn, cum, state)
     grad_k, grad_v = call(
-        final_kernel, "final", [scalars] + [tile] * 4 + [cum_spec, per_head(seq)],
-        [tile] * 2, [flat_bf16, flat_bf16], 7,
-    )(late_weight, k, v, part_k, part_v, cum, passes)
+        final_kernel, "final", [tile] * 4 + [cum_spec, per_head],
+        [tile] * 2, [flat_bf16, flat_bf16], 10,
+    )(k, v, part_k, part_v, cum, later)
     return grad_q[None], grad_k[None], grad_v[None]
 
 

time: 230 us -> 137 us (0.60)
  the two profiles are of different devices: /device:TPU:0 before, /device:TPU:28 now
where the time goes in v2:
time: 137 us; the launch traced here: 135 us
  Pallas kernels  121 us (88%)
  local copies, waits for them, and re-layouts  5.09 us (4%)
  other arithmetic  4.65 us (3%)
  blocking collectives  2.47 us (2%)
  starting transfers between devices  1.64 us (1%)
    pallas_call x1, Pallas kernels, local(): call(functools.partial(back_kernel, seq), 'back', [whole_in] + [tile] * 4...  36.4 us
    pallas_call x1, Pallas kernels, local(): call(functools.partial(intra_kernel, seq), 'intra', [whole_in, tile, tile...  34.6 us
    pallas_call x1, Pallas kernels, project(): pl.pallas_call(functools.partial(project_kernel, tp, last), name='project...  15.1 us
    pallas_call x1, Pallas kernels, local(): call(final_kernel, 'final', [tile] * 4 + [cum_spec, per_head], [tile] * 2...  9.79 us
    pallas_call x1, Pallas kernels, local(): call(norm_kernel, 'norm', [tile, tile, tile, cum_spec, lanes, lanes], [ti...  8.9 us
    pallas_call x1, Pallas kernels, local(): call(inter_kernel, 'inter', [tile, tile, cum_spec, per_head], [tile, lane...  8.56 us
    pallas_call x1, Pallas kernels, local(): call(state_kernel, 'states', [tile, tile, cum_spec], payload_tile, payloa...  7.38 us
  transfers between devices with their start and end apart: 2, of which 0 were waited for; matrix products, arithmetic and copies ran while one was open for 3% of the time, Pallas kernels for 37%

profile of v2, /device:TPU:28, one launch (start us, length us, event | category | flops | bytes accessed | tf_op | source)
XLA Modules:
  0.0 135.4 jit_solution(153997686760910305)
XLA Ops:
  0.6 1.6 %collective-permute-start = (bf16[512,1536]{1,0:T(8,128)(2,1)}, bf16[512,1536]{1,0:T(8,128)(2,1)S(1)}, u32[]{:S(2)}, u32[]{:S(2)}) collective-permute-start(bf16[512,1536]{1,0:T(8,128)(2,1)} %bitcast.39), channel_id=1, source_target_pairs={{0,1},{1,0},{2,3},{3,2},{4,5},{5,4},{6,7},{7,6},{8,9},{9,8},{10,11... | collective-permute-start | bytes 4718600 | tf_op jit(solution)/shard_map/ppermute | solution.py:248
  2.2 0.8 reshape.42
  3.0 1.2 reduce-window.6
  4.1 0.2 slice_reduce_fusion
  4.3 0.7 copy_bitcast_fusion.cum_ref
  5.0 7.4 %states.1.payload_ref = bf16[16,144,128]{2,1,0:T(8,128)(2,1)} custom-call(bf16[512,2048]{1,0:T(8,128)(2,1)} %bitcast.31, bf16[512,2048]{1,0:T(8,128)(2,1)} %bitcast.35, f32[16,512]{1,0:T(8,128)} %copy_bitcast_fusion.cum_ref), custom_call_target="tpu_custom_call" | custom-call | flops 6300000256 | bytes 7000000 | tf_op jit(solution)/shard_map/states/pallas_call | solution.py:314
  12.4 34.6 %intra.1 = (f32[512,2048]{1,0:T(8,128)}, bf16[16,128,128]{2,1,0:T(8,128)(2,1)}) custom-call(bf16[16,144,128]{2,1,0:T(8,128)(2,1)} %states.1.payload_ref, bf16[512,2048]{1,0:T(8,128)(2,1)} %bitcast.27, bf16[512,2048]{1,0:T(8,128)(2,1)} %bitcast.32, bf16[512,2048]{1,0:T(8,128)(2,1)} %bitcast.36, f32[16,512]{1,0:T(8,128)} %copy_bitcast_fusion.cum_ref), custom_call_target="tpu_custom_call" | custom-call | flops 27000000512 | bytes 30000000 | tf_op jit(solution)/shard_map/intra/pallas_call | solution.py:318
  47.0 0.0 collective-permute-done.refs_1_
  47.0 0.0 copy-start.1
  47.0 0.1 collective-permute-start.1
  47.1 8.6 %inter.1 = (f32[512,2048]{1,0:T(8,128)}, f32[512,128]{1,0:T(8,128)}) custom-call(bf16[512,2048]{1,0:T(8,128)(2,1)} %bitcast.28, f32[512,2048]{1,0:T(8,128)} %get-tuple-element.18.intra_ref, f32[16,512]{1,0:T(8,128)} %copy_bitcast_fusion.cum_ref, bf16[16,128,128]{2,1,0:T(8,128)(2,1)} %get-tuple-element.20.state_ref), custom_call_target="tpu_custom_call" | custom-call | flops 8099999744 | bytes 9000000 | tf_op jit(solution)/shard_map/inter/pallas_call | solution.py:322
  55.7 0.0 copy-done.1
  55.7 1.1 reduce_sum.18
  56.8 0.6 pad_add_fusion.refs_0_
  57.4 0.0 collective-permute-done.1.refs_2_
  57.4 0.0 copy-start.2
  57.4 1.1 copy-done.2
  58.5 15.1 %project.1 = (f32[512,2048]{1,0:T(8,128)}, f32[512,128]{1,0:T(8,128)}) custom-call(s32[2]{0:T(128)} %pad_add_fusion.refs_0_, bf16[512,1536]{1,0:T(8,128)(2,1)} %copy-done.1, bf16[512,1536]{1,0:T(8,128)(2,1)} %copy-done.2, bf16[2048,3072]{1,0:T(8,128)(2,1)} %bitcast.19, bf16[2048,3072]{1,0:T(8,128)(2,1)} %bitcast.20, ...), custom_call_target="tpu_custom_call" | custom-call | flops 6442450944 | bytes 16777216 | tf_op jit(solution)/shard_map/project/pallas_call | solution.py:346
  73.6 1.1 reduce_sum.19
  74.7 2.5 %psum.7 = f32[2,512]{1,0:T(2,128)S(1)} all-reduce(f32[2,512]{1,0:T(2,128)S(1)} %pad_maximum_fusion), channel_id=1, replica_groups=mesh['seq'=8,'tp'=2,'pp'=2] {'tp'}, use_global_device_ids=true, to_apply=%region_4.5 | all-reduce | flops 1024 | bytes 8192 | tf_op jit(solution)/shard_map/psum | solution.py:369
  77.2 0.8 broadcast_in_dim.10.inv_ref
  78.0 0.8 broadcast_in_dim.22.fac_ref
  78.9 8.9 %norm.1 = (bf16[512,2048]{1,0:T(8,128)(2,1)}, bf16[16,144,128]{2,1,0:T(8,128)(2,1)}) custom-call(f32[512,2048]{1,0:T(8,128)} %get-tuple-element.22.norm_ref, f32[512,2048]{1,0:T(8,128)} %get-tuple-element.21.refs_5_.att_ref, bf16[512,2048]{1,0:T(8,128)(2,1)} %bitcast.29, f32[16,512]{1,0:T(8,128)} %copy_bitcast_fusion.cum_ref, ...), custom_call_target="tpu_custom_call" | custom-call | flops 8099999744 | bytes 9000000 | tf_op jit(solution)/shard_map/norm/pallas_call | solution.py:374
  87.8 36.4 %back.1 = (bf16[512,2048]{1,0:T(8,128)(2,1)}, f32[512,2048]{1,0:T(8,128)}, f32[512,2048]{1,0:T(8,128)}, bf16[16,128,128]{2,1,0:T(8,128)(2,1)}) custom-call(bf16[16,144,128]{2,1,0:T(8,128)(2,1)} %get-tuple-element.25.payload_ref, bf16[512,2048]{1,0:T(8,128)(2,1)} %bitcast.30, bf16[512,2048]{1,0:T(8,128)(2,1)} %bitcast.33, bf16[512,2048]{1,0:T(8,128)(2,1)} %bitcast.37, ...), custom_call_target="tpu_custom_call" | custom-call | flops 27000000512 | bytes 30000000 | tf_op jit(solution)/shard_map/back/pallas_call | solution.py:378
  124.2 0.0 copy-start
  124.2 9.8 %final.1 = (bf16[512,2048]{1,0:T(8,128)(2,1)}, bf16[512,2048]{1,0:T(8,128)(2,1)}) custom-call(bf16[512,2048]{1,0:T(8,128)(2,1)} %bitcast.34, bf16[512,2048]{1,0:T(8,128)(2,1)} %bitcast.38, f32[512,2048]{1,0:T(8,128)} %get-tuple-element.28.gk_ref, f32[512,2048]{1,0:T(8,128)} %get-tuple-element.29.gv_ref, f32[16,512]{1,0:T(8,128)} %copy_bitcast_fusion.cum_ref, ...), custom_call_target="tpu_custom_call" | custom-call | flops 8999999488 | bytes 10000000 | tf_op jit(solution)/shard_map/final/pallas_call | solution.py:382
  134.0 0.0 copy-done
  134.0 1.3 copy.17
  (6 shorter events, 0.1 us)
Async XLA Ops:
  0.6 46.4 %collective-permute-start = (bf16[512,1536]{1,0:T(8,128)(2,1)}, bf16[512,1536]{1,0:T(8,128)(2,1)S(1)}, u32[]{:S(2)}, u32[]{:S(2)}) collective-permute-start(bf16[512,1536]{1,0:T(8,128)(2,1)} %bitcast.39), channel_id=1, source_target_pairs={{0,1},{1,0},{2,3},{3,2},{4,5},{5,4},{6,7},{7,6},{8,9},{9,8},{10,11... | collective-permute-start | bytes 4718600 | tf_op jit(solution)/shard_map/ppermute | solution.py:248
  47.0 8.7 %copy-start.1 = (bf16[512,1536]{1,0:T(8,128)(2,1)}, bf16[512,1536]{1,0:T(8,128)(2,1)S(1)}, u32[]{:S(2)}) copy-start(bf16[512,1536]{1,0:T(8,128)(2,1)S(1)} %collective-permute-done.refs_1_) | copy-start | bytes 4718596
  47.0 10.3 %collective-permute-start.1 = (bf16[512,1536]{1,0:T(8,128)(2,1)S(1)}, bf16[512,1536]{1,0:T(8,128)(2,1)S(1)}, u32[]{:S(2)}, u32[]{:S(2)}) collective-permute-start(bf16[512,1536]{1,0:T(8,128)(2,1)S(1)} %collective-permute-done.refs_1_), channel_id=1, source_target_pairs={{0,2},{2,0},{1,3},{3,1},{4,6},{6,4},{5,7},{7,5},{8,10},{10,8},{9,1... | collective-permute-start | bytes 4718600 | tf_op jit(solution)/shard_map/ppermute | solution.py:248
  57.4 1.1 copy-start.2
  124.2 9.8 %copy-start = (bf16[512,2048]{1,0:T(8,128)(2,1)S(1)}, bf16[512,2048]{1,0:T(8,128)(2,1)}, u32[]{:S(2)}) copy-start(bf16[512,2048]{1,0:T(8,128)(2,1)} %get-tuple-element.27) | copy-start | bytes 6291460
